TPU v7x, 512 devices: a whole 4x8x8 slice. The times are simulated.
512 devices in a mesh: traj: 4 (over x), slab: 128 (over z, y, core).
Axes of the slice: x: 4, y: 8, z: 8, core: 2. Of those that a mesh axis runs over, the one named last changes fastest.
Arguments:
- grad_out: bfloat16 [1024, 384, 128], P(('traj', 'slab')), parts along dimension 0, may hold values from -96 to 96
- cached: bfloat16 [1024, 384, 128], P('traj', 'slab'), parts along dimension 0, may hold values from -0.059814453 to 0.059814453
- values: bfloat16 [1024, 384, 128], P(('traj', 'slab')), parts along dimension 0, may hold values from -0.75 to 0.75
- query_x: bfloat16 [1024, 128], P('traj'), parts along dimension 0, may hold values from -6 to 6
- key_x: bfloat16 [1024, 128], P('traj'), parts along dimension 0, may hold values from -6 to 6
- query_y: bfloat16 [1536, 128], P('traj'), parts along dimension 0, may hold values from -6 to 6
- key_y: bfloat16 [1536, 128], P('traj'), parts along dimension 0, may hold values from -6 to 6
Outputs:
- grad_values: bfloat16 [1024, 384, 128], P(('traj', 'slab')), parts along dimension 0
- query_x_grad: float32 [1024, 128], P(('traj', 'slab')), parts along dimension 0
- key_x_grad: float32 [1024, 128], P(('traj', 'slab')), parts along dimension 0
- query_y_grad: float32 [1536, 128], P(('traj', 'slab')), parts along dimension 0
- key_y_grad: float32 [1536, 128], P(('traj', 'slab')), parts along dimension 0
There are 4 independent parts, one for each index of `traj`. A program takes and returns all parts, laid end to end along the dimension named above; each array names one. Nothing has to cross between parts.
All inputs are finite; a program needn't handle non-finite values.
Results may differ from a plain program's by a relative error of at most 0.0067.
Values may be sent and summed in bfloat16 or wider, within the bound.
No kernel may reach another device: no remote copies, remote signals or barrier semaphores. Data moves between devices by JAX's collectives and lax.ppermute only.
A program may use at most 64 MiB of HBM per device.

v0:
```python
import math
import jax
import jax.numpy as jnp
from jax import lax
from jax.sharding import PartitionSpec as P

HEADS = 4
HEAD = 32


def axis_kernel(queries, key_rows):
    scores = jnp.dot(queries, key_rows.T, preferred_element_type=jnp.float32) / math.sqrt(HEAD)
    return jax.nn.softmax(scores, axis=1)


def local_terms(kernel, coupling, queries, key_rows):
    row_delta = jnp.sum(kernel * coupling, axis=1)
    weighted = kernel * coupling
    grad_query = jnp.dot(
        weighted, key_rows.astype(jnp.float32), precision=lax.Precision.HIGHEST
    ) / math.sqrt(HEAD)
    grad_key = jnp.dot(
        weighted.T, queries.astype(jnp.float32), precision=lax.Precision.HIGHEST
    ) / math.sqrt(HEAD)
    return (grad_query, grad_key, row_delta)


def corrections(own_rows, own_cols, delta_total, queries, key_rows, start, count):
    own_delta = lax.dynamic_slice_in_dim(delta_total, start, count, 0)
    query_fix = (
        own_delta[:, None]
        * jnp.dot(own_rows, key_rows.astype(jnp.float32), precision=lax.Precision.HIGHEST)
        / math.sqrt(HEAD)
    )
    key_fix = jnp.dot(
        own_cols.T,
        delta_total[:, None] * queries.astype(jnp.float32),
        precision=lax.Precision.HIGHEST,
    ) / math.sqrt(HEAD)
    return (query_fix, key_fix)


def on_device(grad_out, cached, values, query_x, key_x, query_y, key_y):
    index = lax.axis_index("slab")
    x_rows = grad_out.shape[0]
    x_count = cached.shape[0]
    y_rows = cached.shape[1]
    x_start = index * x_rows
    y_start = index * y_rows
    grad_columns = lax.all_to_all(grad_out, "slab", split_axis=1, concat_axis=0, tiled=True)
    mixed_heads = []
    query_terms = []
    key_terms = []
    delta_terms = []
    row_slices = []
    col_slices = []
    for head_index in range(HEADS):
        offset = head_index * HEAD
        head_query = query_x[:, offset : offset + HEAD]
        head_key = key_x[:, offset : offset + HEAD]
        kernel = axis_kernel(head_query, head_key)
        grad_rows = grad_columns[:, :, offset : offset + HEAD].reshape(x_count, y_rows * HEAD)
        saved_rows = cached[:, :, offset : offset + HEAD].reshape(x_count, y_rows * HEAD)
        grad_mixed = lax.dot_general(
            kernel.astype(jnp.bfloat16),
            grad_rows,
            (((0,), (0,)), ((), ())),
            preferred_element_type=jnp.float32,
        ).astype(jnp.bfloat16)
        coupling = lax.dot_general(
            grad_rows, saved_rows, (((1,), (1,)), ((), ())), preferred_element_type=jnp.float32
        )
        grad_query, grad_key, row_delta = local_terms(kernel, coupling, head_query, head_key)
        query_terms.append(grad_query)
        key_terms.append(grad_key)
        delta_terms.append(row_delta)
        row_slices.append(lax.dynamic_slice_in_dim(kernel, x_start, x_rows, 0))
        col_slices.append(lax.dynamic_slice_in_dim(kernel, x_start, x_rows, 1))
        mixed_heads.append(grad_mixed.reshape(x_count, y_rows, HEAD))
    mixed_rows = lax.all_to_all(
        jnp.concatenate(mixed_heads, axis=2), "slab", split_axis=0, concat_axis=1, tiled=True
    )
    x_delta_total = lax.psum(jnp.stack(delta_terms), "slab")
    query_x_grad, key_x_grad = (
        lax.psum_scatter(
            jnp.concatenate(query_terms, axis=1), "slab", scatter_dimension=0, tiled=True
        ),
        lax.psum_scatter(
            jnp.concatenate(key_terms, axis=1), "slab", scatter_dimension=0, tiled=True
        ),
    )
    query_fixes = []
    key_fixes = []
    for head_index in range(HEADS):
        offset = head_index * HEAD
        query_fix, key_fix = corrections(
            row_slices[head_index],
            col_slices[head_index],
            x_delta_total[head_index],
            query_x[:, offset : offset + HEAD],
            key_x[:, offset : offset + HEAD],
            x_start,
            x_rows,
        )
        query_fixes.append(query_fix)
        key_fixes.append(key_fix)
    query_x_grad = query_x_grad - jnp.concatenate(query_fixes, axis=1)
    key_x_grad = key_x_grad - jnp.concatenate(key_fixes, axis=1)
    value_heads = []
    query_terms = []
    key_terms = []
    delta_terms = []
    row_slices = []
    col_slices = []
    for head_index in range(HEADS):
        offset = head_index * HEAD
        head_query = query_y[:, offset : offset + HEAD]
        head_key = key_y[:, offset : offset + HEAD]
        kernel = axis_kernel(head_query, head_key)
        mixed_head = mixed_rows[:, :, offset : offset + HEAD]
        value_head = values[:, :, offset : offset + HEAD]
        grad_value = jnp.einsum(
            "jk,xje->xke",
            kernel.astype(jnp.bfloat16),
            mixed_head,
            preferred_element_type=jnp.float32,
        )
        coupling = jnp.einsum(
            "xje,xke->jk", mixed_head, value_head, preferred_element_type=jnp.float32
        )
        grad_query, grad_key, row_delta = local_terms(kernel, coupling, head_query, head_key)
        query_terms.append(grad_query)
        key_terms.append(grad_key)
        delta_terms.append(row_delta)
        row_slices.append(lax.dynamic_slice_in_dim(kernel, y_start, y_rows, 0))
        col_slices.append(lax.dynamic_slice_in_dim(kernel, y_start, y_rows, 1))
        value_heads.append(grad_value.astype(jnp.bfloat16))
    y_delta_total = lax.psum(jnp.stack(delta_terms), "slab")
    query_y_grad, key_y_grad = (
        lax.psum_scatter(
            jnp.concatenate(query_terms, axis=1), "slab", scatter_dimension=0, tiled=True
        ),
        lax.psum_scatter(
            jnp.concatenate(key_terms, axis=1), "slab", scatter_dimension=0, tiled=True
        ),
    )
    query_fixes = []
    key_fixes = []
    for head_index in range(HEADS):
        offset = head_index * HEAD
        query_fix, key_fix = corrections(
            row_slices[head_index],
            col_slices[head_index],
            y_delta_total[head_index],
            query_y[:, offset : offset + HEAD],
            key_y[:, offset : offset + HEAD],
            y_start,
            y_rows,
        )
        query_fixes.append(query_fix)
        key_fixes.append(key_fix)
    query_y_grad = query_y_grad - jnp.concatenate(query_fixes, axis=1)
    key_y_grad = key_y_grad - jnp.concatenate(key_fixes, axis=1)
    grad_values = jnp.concatenate(value_heads, axis=2)
    return (grad_values, query_x_grad, key_x_grad, query_y_grad, key_y_grad)


def solution(mesh):
    return jax.shard_map(
        on_device,
        mesh=mesh,
        in_specs=(
            P(("traj", "slab"), None, None),
            P("traj", "slab", None),
            P(("traj", "slab"), None, None),
            P("traj", None),
            P("traj", None),
            P("traj", None),
            P("traj", None),
        ),
        out_specs=(
            P(("traj", "slab"), None, None),
            P(("traj", "slab"), None),
            P(("traj", "slab"), None),
            P(("traj", "slab"), None),
            P(("traj", "slab"), None),
        ),
        check_vma=False,
    )
```

profile of v0, /device:TPU:24, one launch (start us, length us, event | category | flops | bytes accessed | tf_op | source)
XLA Modules:
  0.0 825.0 jit_solution(5174410356687245763)
XLA Ops:
  7.2 1.8 copy.95
  9.0 17.7 %all-to-all-start = ((bf16[2,384,128]{2,0,1:T(2,128)(2,1)}), bf16[2,384,128]{2,0,1:T(2,128)(2,1)}, u32[]{:S(2)}, u32[]{:S(2)}) async-start(bf16[2,384,128]{2,0,1:T(2,128)(2,1)} %copy.95), calls=%async_computation | async-start | bytes 393216 | tf_op jit(solution)/shard_map/all_to_all | solution.py:50
  26.7 1.0 fusion.169
  30.4 1.3 dynamic-slice.8
  33.0 1.1 fusion.39
  34.1 0.7 fusion.38
  34.9 0.7 fusion.36
  35.9 0.7 fusion.40
  37.9 1.1 copy.96
  39.0 1.8 fusion.177
  41.2 0.9 convolution_multiply_fusion.22
  42.1 0.8 fusion.178
  43.0 0.9 convolution_multiply_fusion.19
  43.8 0.8 convolution_multiply_fusion.23
  44.7 0.9 fusion.175
  45.6 0.9 convolution_multiply_fusion.16
  46.5 0.9 convolution_multiply_fusion.20
  47.4 1.0 fusion.165
  48.5 0.9 fusion.176
  49.4 0.7 copy-done.14
  50.1 0.9 convolution_multiply_fusion.21
  51.0 1.7 copy.148
  52.6 1.0 convolution_convert_fusion.7
  53.6 1.7 copy.150
  55.3 1.8 convolution_convert_fusion.5
  57.0 1.7 copy.149
  58.7 1.6 convolution_convert_fusion.6
  60.3 1.7 copy.151
  62.0 1.6 convolution_convert_fusion.4
  63.6 1.7 copy.104
  65.2 1.7 copy.102
  66.9 1.7 copy.103
  68.6 0.9 copy.101
  69.5 2.7 pad_maximum_fusion
  72.2 14.0 %all-to-all-start.1 = ((bf16[256,3,128]{2,1,0:T(4,128)(2,1)}), bf16[256,3,128]{2,1,0:T(4,128)(2,1)}, u32[]{:S(2)}, u32[]{:S(2)}) async-start(bf16[256,3,128]{2,1,0:T(4,128)(2,1)} %pad_maximum_fusion), calls=%async_computation.1 | async-start | bytes 524288 | tf_op jit(solution)/shard_map/all_to_all | solution.py:80
  86.4 1.5 pad_maximum_fusion.4
  90.0 0.7 pad_maximum_fusion.5
  90.6 8.0 all-to-all-done.1
  98.7 1.0 copy.105
  99.8 1.5 fusion.164
  101.3 1.1 copy.153
  102.4 0.9 fusion.9
  103.7 1.1 convolution_multiply_fusion.10
  104.9 1.0 convolution_multiply_fusion.14
  105.9 1.1 copy.152
  106.9 0.8 fusion.8
  108.2 1.1 convolution_multiply_fusion.11
  109.3 1.0 convolution_multiply_fusion.15
  110.2 1.1 copy.155
  111.3 0.9 fusion.11
  112.6 1.1 convolution_multiply_fusion.8
  113.7 1.0 convolution_multiply_fusion.12
  114.7 1.1 copy.154
  116.0 0.7 copy-done.12
  117.7 1.0 convolution_multiply_fusion.13
  118.7 0.7 pad_maximum_fusion.1
  119.4 1.7 copy.127
  121.2 0.7 copy-done.31
  121.8 478.3 %all-reduce.4 = (f32[4,256]{1,0:T(4,128)S(1)}, f32[4,384]{1,0:T(4,128)S(1)}) all-reduce(f32[4,256]{1,0:T(4,128)S(1)} %copy-done.31, f32[4,384]{1,0:T(4,128)S(1)} %pad_maximum_fusion.6), channel_id=1, replica_groups=mesh['traj'=4,'slab'=128] {'slab'}, use_global_device_ids=true, to_apply=%region_21.0 | all-reduce | flops 2560 | bytes 20480 | tf_op jit(solution)/shard_map/psum | solution.py:83
  600.5 0.8 convolution_multiply_fusion.35
  607.6 0.7 pad_maximum_fusion.2
  608.5 0.7 pad_maximum_fusion.3
  610.1 204.0 %all-reduce.8.cloned.1.call-done = (f32[256,128]{0,1:T(8,128)}, f32[256,128]{0,1:T(8,128)}, f32[384,128]{0,1:T(8,128)}, f32[384,128]{0,1:T(8,128)}) async-done(((f32[256,128]{0,1:T(8,128)}, f32[256,128]{0,1:T(8,128)}, f32[384,128]{0,1:T(8,128)}, f32[384,128]{0,1:T(8,128)}), (f32[256,128]{0,1:T(8,128)}, f32[256,128]{0,1:T(8,128)}, f32[384,128]{0,1:T(8,128)}, ...) | async-done | bytes 655376
  814.1 1.1 dynamic-slice_subtract_fusion
  (145 shorter events, 20.3 us)
Async XLA Ops:
  9.0 17.7 %copy-start.1 = (bf16[256,128]{1,0:T(8,128)(2,1)S(1)}, bf16[256,128]{1,0:T(8,128)(2,1)}, u32[]{:S(2)}) copy-start(bf16[256,128]{1,0:T(8,128)(2,1)} %param.11) | copy-start | bytes 196612
  9.0 17.7 %copy-start.3 = (bf16[256,128]{1,0:T(8,128)(2,1)S(1)}, bf16[256,128]{1,0:T(8,128)(2,1)}, u32[]{:S(2)}) copy-start(bf16[256,128]{1,0:T(8,128)(2,1)} %param.10) | copy-start | bytes 196612
  9.0 28.9 %all-to-all-start = ((bf16[2,384,128]{2,0,1:T(2,128)(2,1)}), bf16[2,384,128]{2,0,1:T(2,128)(2,1)}, u32[]{:S(2)}, u32[]{:S(2)}) async-start(bf16[2,384,128]{2,0,1:T(2,128)(2,1)} %copy.95), calls=%async_computation | async-start | bytes 393216 | tf_op jit(solution)/shard_map/all_to_all | solution.py:50
  28.2 0.9 copy-start
  28.2 0.9 copy-start.2
  33.0 1.1 copy-start.13
  37.5 1.5 copy-start.4
  40.8 1.2 copy-start.8
  41.2 1.0 copy-start.5
  47.4 1.0 copy-start.6
  49.4 0.7 copy-start.14
  72.2 14.2 %copy-start.28 = (f32[256,32]{0,1:T(8,128)S(1)}, f32[256,32]{0,1:T(8,128)}, u32[]{:S(2)}) copy-start(f32[256,32]{0,1:T(8,128)} %convolution_multiply_fusion.22) | copy-start | bytes 98308
  72.2 26.5 %all-to-all-start.1 = ((bf16[256,3,128]{2,1,0:T(4,128)(2,1)}), bf16[256,3,128]{2,1,0:T(4,128)(2,1)}, u32[]{:S(2)}, u32[]{:S(2)}) async-start(bf16[256,3,128]{2,1,0:T(4,128)(2,1)} %pad_maximum_fusion), calls=%async_computation.1 | async-start | bytes 524288 | tf_op jit(solution)/shard_map/all_to_all | solution.py:80
  86.1 728.0 %all-reduce.8.cloned.1.call-start = ((), (), s32[]{:S(2)}) async-start(), calls=%async_computation.2 | async-start | bytes 1310720
  86.4 1.5 copy-start.33
  86.4 1.5 copy-start.34
  86.4 1.5 copy-start.35
  86.4 2.8 copy-start.15
  87.9 0.7 copy-start.32
  89.2 0.8 copy-start.26
  89.2 0.8 copy-start.27
  102.4 0.9 copy-start.9
  106.9 0.9 copy-start.10
  111.3 0.9 copy-start.11
  115.8 0.9 copy-start.12
  117.6 1.1 copy-start.23
  117.6 1.1 copy-start.24
  117.6 1.1 copy-start.25
  121.2 0.7 copy-start.31
  600.4 1.6 copy-start.7
  606.5 0.8 copy-start.21
  606.5 0.8 copy-start.22
  606.7 0.8 copy-start.19
  606.8 0.8 copy-start.17
  607.6 0.8 copy-start.16
  607.6 0.8 copy-start.18
  607.6 0.9 copy-start.20
  609.3 0.7 copy-start.36
  815.2 1.3 copy-start.30
  816.5 0.9 copy-start.29
Sparse Core Ops, SparseCore 0:
  609.4 204.6 all-reduce.7
where the time goes:
time: 827 us; the launch traced here: 825 us
  blocking collectives  478 us (58%)
  waiting for transfers between devices  212 us (26%)
  matrix products  37.6 us (5%)
  local copies, waits for them, and re-layouts  35.5 us (4%)
  starting transfers between devices  31.9 us (4%)
  between operations  15.8 us (2%)
  other arithmetic  13.5 us (2%)
    psum x1, blocking collectives, on_device(): x_delta_total = lax.psum(jnp.stack(delta_terms), 'slab')  478 us
    unnamed x2, waiting for transfers between devices  204 us
    unnamed x90, local copies, waits for them, and re-layouts  24.8 us
    all_to_all x1, starting transfers between devices, on_device(): lax.all_to_all(grad_out, 'slab', split_axis=1, concat_axis=0, tiled=True)  17.7 us
  transfers between devices with their start and end apart: 3, of which 3 were waited for; matrix products, arithmetic and copies ran while one was open for 1% of the time, Pallas kernels for 0%

commit v1 on v0

--- a/solution.py
+++ b/solution.py
@@ -6,6 +6,10 @@
 
 HEADS = 4
 HEAD = 32
+
+
+def choose_table(mat, axis_name):
+    return jax.lax.all_gather(mat, axis_name=axis_name).sum(axis=0)
 
 
 def axis_kernel(queries, key_rows):
@@ -80,7 +84,7 @@
     mixed_rows = lax.all_to_all(
         jnp.concatenate(mixed_heads, axis=2), "slab", split_axis=0, concat_axis=1, tiled=True
     )
-    x_delta_total = lax.psum(jnp.stack(delta_terms), "slab")
+    x_delta_total = choose_table(jnp.stack(delta_terms), "slab")
     query_x_grad, key_x_grad = (
         lax.psum_scatter(
             jnp.concatenate(query_terms, axis=1), "slab", scatter_dimension=0, tiled=True

time: 827 us -> 617 us (0.75)
  blocking collectives: 478 us -> 293 us
  local copies, waits for them, and re-layouts: 35.5 us -> 19.9 us
    psum x1, blocking collectives: 478 us -> 238 us  [on_device(): y_delta_total = lax.psum(jnp.stack(delta_terms), 'slab')]
    all_gather x0 -> x1, blocking collectives: none -> 55 us  [choose_table(): return jax.lax.all_gather(mat, axis_name=axis_name).sum(axis=0)]
    unnamed x90 -> x88, local copies, waits for them, and re-layouts: 24.8 us -> 15.5 us
  transfers between devices with their start and end apart: 3 -> 3, of which waited for: 3 -> 3; matrix products, arithmetic and copies ran while one was open for 1% -> 2% of each run, Pallas kernels for 0% -> 0%
where the time goes in v1:
time: 617 us; the launch traced here: 616 us
  blocking collectives  293 us (47%)
  waiting for transfers between devices  214 us (35%)
  matrix products  31.2 us (5%)
  starting transfers between devices  28.6 us (5%)
  local copies, waits for them, and re-layouts  19.9 us (3%)
  between operations  15.9 us (3%)
  other arithmetic  13.2 us (2%)
    psum x1, blocking collectives, on_device(): y_delta_total = lax.psum(jnp.stack(delta_terms), 'slab')  238 us
    unnamed x2, waiting for transfers between devices  204 us
    all_gather x1, blocking collectives, choose_table(): return jax.lax.all_gather(mat, axis_name=axis_name).sum(axis=0)  55 us
    all_to_all x1, starting transfers between devices, on_device(): lax.all_to_all(grad_out, 'slab', split_axis=1, concat_axis=0, tiled=True)  17.7 us
    unnamed x88, local copies, waits for them, and re-layouts  15.5 us
  transfers between devices with their start and end apart: 3, of which 3 were waited for; matrix products, arithmetic and copies ran while one was open for 2% of the time, Pallas kernels for 0%

profile of v1, /device:TPU:24, one launch (start us, length us, event | category | flops | bytes accessed | tf_op | source)
XLA Modules:
  0.0 616.1 jit_solution(17706471264998881810)
XLA Ops:
  7.2 1.8 copy.95
  9.0 17.7 %all-to-all-start = ((bf16[2,384,128]{2,0,1:T(2,128)(2,1)}), bf16[2,384,128]{2,0,1:T(2,128)(2,1)}, u32[]{:S(2)}, u32[]{:S(2)}) async-start(bf16[2,384,128]{2,0,1:T(2,128)(2,1)} %copy.95), calls=%async_computation | async-start | bytes 393216 | tf_op jit(solution)/shard_map/all_to_all | solution.py:54
  27.0 0.9 fusion.170
  28.5 0.6 copy-done
  30.5 1.3 dynamic-slice.8
  33.1 1.0 fusion.38
  34.2 0.7 fusion.36
  35.1 0.7 fusion.42
  35.9 0.8 fusion.40
  37.9 1.1 copy.96
  39.4 0.9 convolution_multiply_fusion.18
  40.6 0.6 copy-done.5
  41.5 0.9 convolution_multiply_fusion.19
  42.4 0.8 convolution_multiply_fusion.23
  43.7 0.9 convolution_multiply_fusion.16
  44.6 0.9 convolution_multiply_fusion.20
  45.5 1.0 fusion.165
  46.9 0.7 copy-done.12
  47.6 0.9 convolution_multiply_fusion.21
  48.5 55.0 %all-gather.1 = f32[128,4,256]{2,1,0:T(4,128)} all-gather(f32[1,4,256]{2,1,0:T(4,128)S(1)} %maximum_bitcast_fusion), channel_id=2, replica_groups=mesh['traj'=4,'slab'=128] {'slab'}, dimensions={0}, use_global_device_ids=true | all-gather | bytes 528384 | tf_op jit(solution)/shard_map/all_gather | solution.py:12
  103.5 1.2 reduce_sum.165
  104.7 0.9 convolution_multiply_fusion.34
  105.7 0.8 convolution_multiply_fusion.35
  106.5 0.9 fusion.19
  107.4 0.9 fusion.18
  108.3 0.9 convolution_multiply_fusion.33
  109.2 0.9 convolution_multiply_fusion.32
  110.1 0.9 fusion.17
  111.0 0.9 fusion.16
  112.0 1.0 copy.148
  113.2 1.0 copy.150
  114.2 1.2 convolution_convert_fusion.5
  115.5 0.8 convolution_convert_fusion.6
  117.0 0.6 copy-done.18
  118.0 0.9 copy.101
  118.8 2.5 pad_maximum_fusion
  121.3 10.7 %all-to-all-start.1 = ((bf16[256,3,128]{2,1,0:T(4,128)(2,1)}), bf16[256,3,128]{2,1,0:T(4,128)(2,1)S(1)}, u32[]{:S(2)}, u32[]{:S(2)}) async-start(bf16[256,3,128]{2,1,0:T(4,128)(2,1)} %pad_maximum_fusion), calls=%async_computation.1 | async-start | bytes 524288 | tf_op jit(solution)/shard_map/all_to_all | solution.py:84
  132.4 0.7 pad_maximum_fusion.4
  133.2 0.6 copy-done.28
  134.9 0.7 pad_maximum_fusion.5
  135.5 9.4 %all-to-all-done.1 = bf16[256,3,128]{2,1,0:T(4,128)(2,1)S(1)} async-done(((bf16[256,3,128]{2,1,0:T(4,128)(2,1)}), bf16[256,3,128]{2,1,0:T(4,128)(2,1)S(1)}, u32[]{:S(2)}, u32[]{:S(2)}) %all-to-all-start.1) | async-done | bytes 196640 | tf_op jit(solution)/shard_map/all_to_all | solution.py:84
  145.1 0.8 fusion.164
  146.0 0.9 fusion.9
  147.4 1.1 convolution_multiply_fusion.10
  148.5 1.0 convolution_multiply_fusion.14
  149.6 0.8 fusion.8
  150.8 0.5 convolution_multiply_fusion.11
  152.0 0.4 fusion.179
  152.4 0.5 convolution_multiply_fusion.8
  153.6 0.4 fusion.180
  154.1 0.5 convolution_multiply_fusion.9
  155.4 0.8 copy.127
  156.3 238.2 %psum.7 = f32[4,384]{1,0:T(4,128)S(1)} all-reduce(f32[4,384]{1,0:T(4,128)S(1)} %pad_maximum_fusion.6), channel_id=1, replica_groups=mesh['traj'=4,'slab'=128] {'slab'}, use_global_device_ids=true, to_apply=%region_28.0 | all-reduce | flops 1536 | bytes 12288 | tf_op jit(solution)/shard_map/psum | solution.py:142
  395.9 0.4 fusion.14
  397.6 0.6 copy-done.17
  398.2 0.7 pad_maximum_fusion.2
  399.0 0.7 pad_maximum_fusion.3
  400.3 204.2 %all-reduce.7.cloned.1.call-done = (f32[256,128]{0,1:T(8,128)}, f32[256,128]{0,1:T(8,128)}, f32[384,128]{0,1:T(8,128)}, f32[384,128]{0,1:T(8,128)}) async-done(((f32[256,128]{0,1:T(8,128)}, f32[256,128]{0,1:T(8,128)}, f32[384,128]{0,1:T(8,128)}, f32[384,128]{0,1:T(8,128)}), (f32[256,128]{0,1:T(8,128)}, f32[256,128]{0,1:T(8,128)}, f32[384,128]{0,1:T(8,128)}, ...) | async-done | bytes 655376
  604.6 1.0 dynamic-slice_subtract_fusion.2
  605.5 0.6 copy.129
  606.3 0.6 copy.128
  606.9 1.1 dynamic-slice_subtract_fusion
  608.0 0.7 copy.131
  608.6 0.7 copy.130
  (145 shorter events, 15.4 us)
Async XLA Ops:
  9.0 17.7 %copy-start.1 = (bf16[256,128]{1,0:T(8,128)(2,1)S(1)}, bf16[256,128]{1,0:T(8,128)(2,1)}, u32[]{:S(2)}) copy-start(bf16[256,128]{1,0:T(8,128)(2,1)} %param.11) | copy-start | bytes 196612
  9.0 17.7 %copy-start.3 = (bf16[256,128]{1,0:T(8,128)(2,1)S(1)}, bf16[256,128]{1,0:T(8,128)(2,1)}, u32[]{:S(2)}) copy-start(bf16[256,128]{1,0:T(8,128)(2,1)} %param.10) | copy-start | bytes 196612
  9.0 28.9 %all-to-all-start = ((bf16[2,384,128]{2,0,1:T(2,128)(2,1)}), bf16[2,384,128]{2,0,1:T(2,128)(2,1)}, u32[]{:S(2)}, u32[]{:S(2)}) async-start(bf16[2,384,128]{2,0,1:T(2,128)(2,1)} %copy.95), calls=%async_computation | async-start | bytes 393216 | tf_op jit(solution)/shard_map/all_to_all | solution.py:54
  27.0 6.0 copy-start.11
  28.2 0.9 copy-start
  28.2 0.9 copy-start.2
  33.1 1.0 copy-start.10
  37.9 1.1 copy-start.8
  40.3 0.9 copy-start.5
  42.4 0.9 copy-start.4
  45.5 1.0 copy-start.6
  46.9 0.7 copy-start.12
  105.6 2.7 copy-start.7
  114.2 1.2 copy-start.15
  115.5 0.9 copy-start.14
  116.8 0.8 copy-start.18
  121.3 11.0 %copy-start.24 = (f32[256,32]{0,1:T(8,128)S(1)}, f32[256,32]{0,1:T(8,128)}, u32[]{:S(2)}) copy-start(f32[256,32]{0,1:T(8,128)} %convolution_multiply_fusion.23) | copy-start | bytes 98308
  121.3 11.0 %copy-start.25 = (f32[256,32]{0,1:T(8,128)S(1)}, f32[256,32]{0,1:T(8,128)}, u32[]{:S(2)}) copy-start(f32[256,32]{0,1:T(8,128)} %convolution_multiply_fusion.20) | copy-start | bytes 98308
  121.3 11.1 %copy-start.26 = (f32[256,32]{0,1:T(8,128)S(1)}, f32[256,32]{0,1:T(8,128)}, u32[]{:S(2)}) copy-start(f32[256,32]{0,1:T(8,128)} %convolution_multiply_fusion.21) | copy-start | bytes 98308
  121.3 11.7 %copy-start.32 = (f32[2,32]{1,0:T(2,128)S(1)}, f32[2,32]{1,0:T(2,128)}, u32[]{:S(2)}) copy-start(f32[2,32]{1,0:T(2,128)} %convolution_multiply_fusion.34) | copy-start | bytes 772
  121.3 11.7 %copy-start.33 = (f32[2,32]{1,0:T(2,128)S(1)}, f32[2,32]{1,0:T(2,128)}, u32[]{:S(2)}) copy-start(f32[2,32]{1,0:T(2,128)} %convolution_multiply_fusion.35) | copy-start | bytes 772
  121.3 11.7 %copy-start.34 = (f32[2,32]{1,0:T(2,128)S(1)}, f32[2,32]{1,0:T(2,128)}, u32[]{:S(2)}) copy-start(f32[2,32]{1,0:T(2,128)} %convolution_multiply_fusion.33) | copy-start | bytes 772
  121.3 11.7 %copy-start.35 = (f32[2,32]{1,0:T(2,128)S(1)}, f32[2,32]{1,0:T(2,128)}, u32[]{:S(2)}) copy-start(f32[2,32]{1,0:T(2,128)} %convolution_multiply_fusion.32) | copy-start | bytes 772
  121.3 23.6 %all-to-all-start.1 = ((bf16[256,3,128]{2,1,0:T(4,128)(2,1)}), bf16[256,3,128]{2,1,0:T(4,128)(2,1)S(1)}, u32[]{:S(2)}, u32[]{:S(2)}) async-start(bf16[256,3,128]{2,1,0:T(4,128)(2,1)} %pad_maximum_fusion), calls=%async_computation.1 | async-start | bytes 524288 | tf_op jit(solution)/shard_map/all_to_all | solution.py:84
  132.0 2.0 copy-start.13
  132.1 472.5 %all-reduce.7.cloned.1.call-start = ((), (), s32[]{:S(2)}) async-start(), calls=%async_computation.2 | async-start | bytes 1310720
  133.0 0.7 copy-start.28
  133.0 0.7 copy-start.29
  133.1 0.7 copy-start.30
  133.1 0.7 copy-start.31
  134.1 0.8 copy-start.21
  134.1 0.8 copy-start.22
  134.1 0.8 copy-start.23
  146.0 0.9 copy-start.9
  154.6 0.8 copy-start.19
  154.6 0.8 copy-start.20
  397.4 0.8 copy-start.17
  398.2 0.8 copy-start.16
  604.6 1.6 copy-start.27
Sparse Core Ops, SparseCore 0:
  399.8 204.6 all-reduce.6
